TPU v7x, 512 devices: a whole 4x8x8 slice. The times are simulated.
512 devices in a mesh: tm: 64 (over z, x, core), band: 8 (over y).
Axes of the slice: x: 4, y: 8, z: 8, core: 2. Of those that a mesh axis runs over, the one named last changes fastest.
Arguments:
- query_input: bfloat16 [64, 40, 26, 1120], P('tm', 'band'), may hold values from -6 to 6
- key_input: bfloat16 [64, 40, 26, 1120], P('tm', 'band'), may hold values from -8 to 8
- value_input: bfloat16 [64, 40, 26, 1120], P('tm', 'band'), may hold values from -12 to 12
- cotangent: bfloat16 [64, 40, 26, 1120], P('tm', 'band'), may hold values from -6 to 6
- local_kernel_weight: float32 [3, 3, 1120], replicated, may hold values from -2 to 2
Outputs:
- mixed_out: bfloat16 [64, 40, 26, 1120], P('tm', 'band')
- query_grad: bfloat16 [64, 40, 26, 1120], P('tm', 'band')
- key_grad: bfloat16 [64, 40, 26, 1120], P('tm', 'band')
- value_grad: bfloat16 [64, 40, 26, 1120], P('tm', 'band')
- kernel_grad: float32 [3, 3, 1120], replicated
All inputs are finite; a program needn't handle non-finite values.
Results may differ from a plain program's by a relative error of at most 0.018.
Values may be sent and summed in bfloat16 or wider, within the bound.
No kernel may reach another device: no remote copies, remote signals or barrier semaphores. Data moves between devices by JAX's collectives and lax.ppermute only.
A program may use at most 128 MiB of HBM per device.

v0:
```python
import math
import jax
import jax.numpy as jnp
from jax import lax
from jax.sharding import PartitionSpec as P

HEADS = 35
HEAD_DIM = 32


def entering(shard, axis, combine, identity, reverse):
    devices, mine = (lax.axis_size(axis), lax.axis_index(axis))
    everything = jax.tree.map(lambda part: lax.all_gather(part, axis), shard)
    start = jax.tree.map(
        lambda part, zero: jnp.broadcast_to(jnp.asarray(zero, part.dtype), part.shape),
        shard,
        identity,
    )

    def step(k, before):
        at = devices - 1 - k if reverse else k
        reached = at > mine if reverse else at < mine
        new = combine(before, jax.tree.map(lambda part: part[at], everything))
        return jax.tree.map(lambda a, b: jnp.where(reached, a, b), new, before)

    return lax.fori_loop(0, devices, step, start)


def padded(cells, sides, width):
    for axis, dim in sides:
        count = lax.axis_size(axis)
        ends = count - 1
        head = lax.slice_in_dim(cells, 0, width, axis=dim)
        tail = lax.slice_in_dim(cells, cells.shape[dim] - width, cells.shape[dim], axis=dim)
        cells = jnp.concatenate(
            [
                lax.ppermute(tail, axis, [(i, (i + 1) % count) for i in range(ends)]),
                cells,
                lax.ppermute(head, axis, [((i + 1) % count, i) for i in range(ends)]),
            ],
            axis=dim,
        )
    return cells


def feature(x):
    return jnp.where(x > 0, x + 1.0, jnp.exp(jnp.minimum(x, 0.0)))


def slope(x):
    return jnp.where(x > 0, jnp.ones_like(x), jnp.exp(jnp.minimum(x, 0.0)))


def add_pair(earlier, later_term):
    return (earlier[0] + later_term[0], earlier[1] + later_term[1])


def frame_totals(terms, backward):
    frame = lax.psum(terms, "band")
    start = (jnp.zeros_like(frame[0]), jnp.zeros_like(frame[1]))
    before = entering(frame, "tm", add_pair, start, backward)
    return add_pair(before, frame)


def group_heads_count():
    chosen = 1
    for candidate in range(1, HEADS + 1):
        if HEADS % candidate == 0 and candidate * HEAD_DIM <= 256:
            chosen = candidate
    return chosen


def block_outer(left, right, group_count, group_heads, precise):
    count = left.shape[0]
    group_width = group_heads * HEAD_DIM
    left_groups = left.reshape(count, group_count, group_width)
    right_groups = right.reshape(count, group_count, group_width)
    if precise:
        whole = jnp.einsum(
            "tga,tgb->gab", left_groups, right_groups, precision=lax.Precision.HIGHEST
        )
    else:
        whole = jnp.einsum(
            "tga,tgb->gab", left_groups, right_groups, preferred_element_type=jnp.float32
        )
    whole = whole.reshape(group_count, group_heads, HEAD_DIM, group_heads, HEAD_DIM)
    same_head = jnp.eye(group_heads, dtype=jnp.float32)[None, :, None, :, None]
    return jnp.sum(whole * same_head, axis=3).reshape(HEADS, HEAD_DIM, HEAD_DIM)


def block_matrix(state, group_count, group_heads):
    group_width = group_heads * HEAD_DIM
    placed = state.reshape(group_count, group_heads, HEAD_DIM, 1, HEAD_DIM)
    same_head = jnp.eye(group_heads, dtype=jnp.float32)[None, :, None, :, None]
    return (placed * same_head).reshape(group_count, group_width, group_width)


def apply_blocks(rows, blocks, transposed):
    count = rows.shape[0]
    group_count, group_width = (blocks.shape[0], blocks.shape[1])
    grouped = rows.reshape(count, group_count, group_width)
    if transposed:
        result = jnp.einsum("tgb,gab->tga", grouped, blocks, precision=lax.Precision.HIGHEST)
    else:
        result = jnp.einsum("tga,gab->tgb", grouped, blocks, precision=lax.Precision.HIGHEST)
    return result.reshape(count, group_count * group_width)


def shards(query_input, key_input, value_input, cotangent, local_kernel_weight):
    high = lax.Precision.HIGHEST
    band_row_span, column_count, width = (
        query_input.shape[1],
        query_input.shape[2],
        query_input.shape[3],
    )
    count = band_row_span * column_count
    group_heads = group_heads_count()
    group_count = HEADS // group_heads
    indicator = (jnp.arange(width)[:, None] // HEAD_DIM == jnp.arange(HEADS)[None, :]).astype(
        jnp.float32
    )
    q_raw = query_input[0].reshape(count, width).astype(jnp.float32)
    k_raw = key_input[0].reshape(count, width).astype(jnp.float32)
    q_feat = feature(q_raw).astype(jnp.bfloat16)
    k_feat = feature(k_raw).astype(jnp.bfloat16)
    value_flat = value_input[0].reshape(count, width)
    own_state = block_outer(k_feat, value_flat, group_count, group_heads, False)
    own_norm = jnp.sum(k_feat, axis=0, dtype=jnp.float32).reshape(HEADS, HEAD_DIM)
    state, norm_vec = frame_totals((own_state, own_norm), False)
    q_wide = q_feat.astype(jnp.float32)
    state_blocks = block_matrix(state, group_count, group_heads)
    norm_flat = norm_vec.reshape(width)
    num = apply_blocks(q_wide, state_blocks, False)
    den = jnp.dot(q_wide * norm_flat, indicator, precision=high)
    den_wide = jnp.dot(den, indicator.T, precision=high)
    attn = num / den_wide
    stacked = jnp.stack([value_input[0], cotangent[0]])
    rimmed = padded(stacked, (("band", 1),), 1)
    padded_input = jnp.pad(rimmed, ((0, 0), (0, 0), (1, 1), (0, 0)))
    value_padded = padded_input[0]
    gpad = padded_input[1]
    complete_gradient = cotangent[0].astype(jnp.float32)
    local_output = jnp.zeros((band_row_span, column_count, width), jnp.float32)
    v_local = jnp.zeros((band_row_span, column_count, width), jnp.float32)
    kernel_row_slice = []
    for row_offset in range(3):
        for column_offset in range(3):
            local_output = (
                local_output
                + local_kernel_weight[row_offset, column_offset]
                * value_padded[
                    row_offset : row_offset + band_row_span,
                    column_offset : column_offset + column_count,
                ]
            )
            v_local = (
                v_local
                + local_kernel_weight[row_offset, column_offset]
                * gpad[
                    2 - row_offset : 2 - row_offset + band_row_span,
                    2 - column_offset : 2 - column_offset + column_count,
                ]
            )
            kernel_row_slice.append(
                jnp.sum(
                    complete_gradient
                    * value_padded[
                        row_offset : row_offset + band_row_span,
                        column_offset : column_offset + column_count,
                    ],
                    axis=(0, 1),
                )
            )
    mixed_out = (attn.reshape(band_row_span, column_count, width) + local_output).astype(
        jnp.bfloat16
    )[None]
    grad_flat = complete_gradient.reshape(count, width)
    scaled = grad_flat / den_wide
    den_grad = -jnp.dot(grad_flat * attn, indicator, precision=high) / den
    den_grad_wide = jnp.dot(den_grad, indicator.T, precision=high)
    back_state = block_outer(q_wide, scaled, group_count, group_heads, True)
    back_norm = jnp.sum(q_wide * den_grad_wide, axis=0).reshape(HEADS, HEAD_DIM)
    later_state, later_norm = frame_totals((back_state, back_norm), True)
    query_grad = apply_blocks(scaled, state_blocks, True) + den_grad_wide * norm_flat
    query_grad = (
        (query_grad * slope(q_raw))
        .reshape(band_row_span, column_count, width)
        .astype(jnp.bfloat16)[None]
    )
    later_blocks = block_matrix(later_state, group_count, group_heads)
    key_grad = apply_blocks(
        value_flat.astype(jnp.float32), later_blocks, True
    ) + later_norm.reshape(width)
    key_grad = (
        (key_grad * slope(k_raw))
        .reshape(band_row_span, column_count, width)
        .astype(jnp.bfloat16)[None]
    )
    value_grad = apply_blocks(k_feat.astype(jnp.float32), later_blocks, False)
    value_grad = (value_grad.reshape(band_row_span, column_count, width) + v_local).astype(
        jnp.bfloat16
    )[None]
    kernel_terms = jnp.stack(kernel_row_slice).reshape(3, 3, width)
    kernel_total = lax.psum(kernel_terms, ("tm", "band"))
    total_tokens = lax.axis_size("tm") * lax.axis_size("band") * count
    kernel_grad = kernel_total / math.sqrt(total_tokens)
    return (mixed_out, query_grad, key_grad, value_grad, kernel_grad)


def solution(mesh):
    placed = (
        P("tm", "band", None, None),
        P("tm", "band", None, None),
        P("tm", "band", None, None),
        P("tm", "band", None, None),
        P(),
    )
    return jax.shard_map(
        shards,
        mesh=mesh,
        in_specs=placed,
        out_specs=(
            P("tm", "band", None, None),
            P("tm", "band", None, None),
            P("tm", "band", None, None),
            P("tm", "band", None, None),
            P(),
        ),
        check_vma=False,
    )
```

profile of v0, /device:TPU:1, one launch (start us, length us, event | category | flops | bytes accessed | tf_op | source)
XLA Modules:
  0.0 863.7 jit_solution(13523367854085724787)
XLA Ops:
  10.0 2.6 reshape.180
  12.5 4.8 multiply_reduce_fusion.1
  17.4 79.9 %all-reduce.4.cloned.1.call-done = f32[35,32,32]{2,1,0:T(8,128)} async-done(((f32[35,32,32]{2,1,0:T(8,128)}), f32[35,32,32]{2,1,0:T(8,128)}) %all-reduce.4.cloned.1.call-update) | async-done | bytes 143376 | tf_op jit(solution)/shard_map/psum | solution.py:59
  97.5 22.3 %psum.36 = f32[35,32]{1,0:T(8,128)S(1)} all-reduce(f32[35,32]{1,0:T(8,128)S(1)} %reshape.182), channel_id=1, replica_groups=mesh['tm'=64,'band'=8] {'band'}, use_global_device_ids=true, to_apply=%region_3.4 | all-reduce | flops 1120 | bytes 8960 | tf_op jit(solution)/shard_map/psum | solution.py:59
  123.8 69.4 %all-gather.4 = f32[64,35,32]{1,2,0:T(8,128)} all-gather(f32[1,35,32]{1,2,0:T(8,128)S(1)} %copy.44), channel_id=3, replica_groups=mesh['tm'=64,'band'=8] {'tm'}, dimensions={0}, use_global_device_ids=true | all-gather | bytes 291200 | tf_op jit(solution)/shard_map/all_gather | solution.py:13
  193.2 69.6 %all-gather.9.cloned.1.call-done = f32[2240,32,32]{2,1,0:T(8,128)} async-done(((f32[35,32,32]{2,1,0:T(8,128)}), f32[2240,32,32]{2,1,0:T(8,128)}) %all-gather.9.cloned.1.call-update) | async-done | bytes 9175056 | tf_op jit(solution)/shard_map/all_gather | solution.py:13
  262.8 135.1 %while.34 = (s32[]{:T(128)}, f32[35,32,32]{2,1,0:T(8,128)S(1)}, f32[35,32]{1,0:T(8,128)S(1)}, s32[]{:T(128)}, f32[64,35,32,32]{3,2,1,0:T(8,128)}, /*index=5*/f32[64,35,32]{1,2,0:T(8,128)}, s32[]{:T(128)}, s32[]{:T(128)}) while((s32[]{:T(128)}, f32[35,32,32]{2,1,0:T(8,128)S(1)}, f32[35,32]{1,0:T(8,128)S(1)}, s32[]{:T(128)}, ...), condition=%wide.region_5.6_spmd.clone, body=%wide.region_4.5_spmd.clone.sunk | while | flops 110884 | bytes 461555 | solution.py:26
  398.0 2.4 mul.264
  400.4 3.6 mul.265
  405.9 2.4 reshape.183
  409.2 3.0 fusion.73
  412.2 1.5 reshape.185
  413.7 2.0 fusion.49
  415.7 3.9 reshape.187
  419.6 4.8 multiply_reduce_fusion
  424.4 70.0 %all-reduce.6.cloned.1.call-done = f32[35,32,32]{2,1,0:T(8,128)} async-done(((f32[35,32,32]{2,1,0:T(8,128)}), f32[35,32,32]{2,1,0:T(8,128)}) %all-reduce.6.cloned.1.call-update) | async-done | bytes 143376 | tf_op jit(solution)/shard_map/psum | solution.py:59
  494.6 3.2 collective-permute-start
  497.8 1.5 collective-permute-start.1
  499.3 2.0 select_n.142
  501.4 2.2 collective-permute-done.1
  503.6 1.5 fusion.10
  506.2 107.4 %psum.39 = f32[3,3,1120]{2,1,0:T(4,128)S(1)} all-reduce(f32[3,3,1120]{2,1,0:T(4,128)S(1)} %reshape.191), channel_id=1, replica_groups=mesh['tm'=64,'band'=8] {'tm','band'}, use_global_device_ids=true, to_apply=%region_21.22 | all-reduce | flops 10080 | bytes 80640 | tf_op jit(solution)/shard_map/psum | solution.py:204
  614.3 3.1 convolution_bitcast_fusion.3
  618.8 2.1 reshape.184
  620.9 2.2 fusion.4
  624.0 24.1 %psum.38 = f32[35,32]{1,0:T(8,128)S(1)} all-reduce(f32[35,32]{1,0:T(8,128)S(1)} %reshape.189), channel_id=1, replica_groups=mesh['tm'=64,'band'=8] {'band'}, use_global_device_ids=true, to_apply=%region_9.10 | all-reduce | flops 1120 | bytes 8960 | tf_op jit(solution)/shard_map/psum | solution.py:59
  649.0 58.1 %all-gather.5 = f32[64,35,32]{1,2,0:T(8,128)} all-gather(f32[1,35,32]{1,2,0:T(8,128)S(1)} %copy.52), channel_id=5, replica_groups=mesh['tm'=64,'band'=8] {'tm'}, dimensions={0}, use_global_device_ids=true | all-gather | bytes 291200 | tf_op jit(solution)/shard_map/all_gather | solution.py:13
  708.4 135.5 %while.35 = (s32[]{:T(128)}, f32[35,32,32]{2,1,0:T(8,128)S(1)}, f32[35,32]{1,0:T(8,128)S(1)}, s32[]{:T(128)}, f32[64,35,32,32]{3,2,1,0:T(8,128)}, /*index=5*/f32...) while((s32[]{:T(128)}, f32[35,32,32]{2,1,0:T(8,128)S(1)}, ...), condition=%wide.region_11.12_spmd.clone, body=%wide.region_10.11_spmd.clone.sunk | while | flops 110888 | bytes 461617 | solution.py:26
  844.0 2.4 mul.306
  846.4 3.6 mul.307
  851.1 1.8 convolution_bitcast_fusion.1
  854.8 1.4 fusion.53
  (624 shorter events, 287.4 us)
Async XLA Ops:
  7.2 1.8 copy-start.17
  7.2 90.1 %all-reduce.4.cloned.1.call-start = ((), (), s32[]{:S(2)}) async-start(), calls=%async_computation | async-start | bytes 1146880 | tf_op jit(solution)/shard_map/psum | solution.py:59
  9.0 1.0 copy-start.5
  9.5 3.0 copy-start.7
  17.4 245.4 %all-gather.9.cloned.1.call-start = ((), (), s32[]{:S(2)}) async-start(), calls=%async_computation.2 | async-start | bytes 37273600 | tf_op jit(solution)/shard_map/all_gather | solution.py:13
  97.3 22.9 %copy-start.20 = (bf16[1,5,26,1120]{3,2,1,0:T(8,128)(2,1)S(1)}, bf16[1,5,26,1120]{3,2,1,0:T(8,128)(2,1)}, u32[]{:S(2)}) copy-start(bf16[1,5,26,1120]{3,2,1,0:T(8,128)(2,1)} %param.9) | copy-start | bytes 873604
  97.3 397.1 %all-reduce.6.cloned.1.call-start = ((), (), s32[]{:S(2)}) async-start(), calls=%async_computation.1 | async-start | bytes 1146880 | tf_op jit(solution)/shard_map/psum | solution.py:59
  121.4 1.4 copy-start.3
  122.7 285.6 %copy-start.1 = (f32[130,1120]{1,0:T(8,128)}, f32[130,1120]{1,0:T(8,128)S(1)}, u32[]{:S(2)}) copy-start(f32[130,1120]{1,0:T(8,128)S(1)} %reshape.192) | copy-start | bytes 1747204
  262.8 135.1 %copy-start.16 = (f32[35,32,32]{2,1,0:T(8,128)S(1)}, f32[35,32,32]{2,1,0:T(8,128)}, u32[]{:S(2)}) copy-start(f32[35,32,32]{2,1,0:T(8,128)} %all-reduce.4.cloned.1.call-done) | copy-start | bytes 430084
  400.4 3.6 copy-start.9
  412.2 1.5 copy-start.10
  413.7 5.8 copy-start
  424.4 70.1 %copy-start.18 = (bf16[1,5,26,1120]{3,2,1,0:T(8,128)(2,1)S(1)}, bf16[1,5,26,1120]{3,2,1,0:T(8,128)(2,1)}, u32[]{:S(2)}) copy-start(bf16[1,5,26,1120]{3,2,1,0:T(8,128)(2,1)} %param.11) | copy-start | bytes 873604
  424.4 284.0 %all-gather.11.cloned.1.call-start = ((), (), s32[]{:S(2)}) async-start(), calls=%async_computation.3 | async-start | bytes 37273600 | tf_op jit(solution)/shard_map/all_gather | solution.py:13
  494.5 3.2 copy-start.12
  494.5 6.8 copy-start.21
  494.6 6.9 collective-permute-start
  497.8 5.9 collective-permute-start.1
  618.8 4.3 copy-start.2
  620.9 2.2 copy-start.13
  620.9 2.2 copy-start.14
  623.9 83.1 %copy-start.4 = (f32[5,26,1120]{2,1,0:T(8,128)S(1)}, f32[5,26,1120]{2,1,0:T(8,128)}, u32[]{:S(2)}) copy-start(f32[5,26,1120]{2,1,0:T(8,128)} %reshape.184) | copy-start | bytes 1747204
  708.4 135.5 %copy-start.15 = (f32[35,32,32]{2,1,0:T(8,128)S(1)}, f32[35,32,32]{2,1,0:T(8,128)}, u32[]{:S(2)}) copy-start(f32[35,32,32]{2,1,0:T(8,128)} %all-reduce.6.cloned.1.call-done) | copy-start | bytes 430084
  846.4 3.6 copy-start.6
  850.0 1.0 copy-start.8
  853.1 1.1 copy-start.11
  854.8 1.4 copy-start.19
Sparse Core Ops, SparseCore 0:
  17.5 79.7 all-reduce.3
  100.6 162.1 all-gather.8
  424.5 69.8 all-reduce.5
  497.6 161.7 all-gather.10
where the time goes:
time: 877 us; the launch traced here: 864 us
  blocking collectives  281 us (32%)
  waiting for transfers between devices  222 us (25%)
  other arithmetic  182 us (21%)
  local copies, waits for them, and re-layouts  141 us (16%)
  matrix products  15.3 us (2%)
  between operations  14.3 us (2%)
    select_n x256, other arithmetic, step(): return jax.tree.map(lambda a, b: jnp.where(reached, a, b), new, before)  163 us
    psum x2, waiting for transfers between devices, frame_totals(): frame = lax.psum(terms, 'band')  150 us
    all_gather x2, blocking collectives, entering(): everything = jax.tree.map(lambda part: lax.all_gather(part, axis), shard)  127 us
    psum x1, blocking collectives, shards(): kernel_total = lax.psum(kernel_terms, ('tm', 'band'))  107 us
    dynamic_slice x256, local copies, waits for them, and re-layouts, step(): new = combine(before, jax.tree.map(lambda part: part[at], everything))  104 us
    all_gather x2, waiting for transfers between devices, entering(): everything = jax.tree.map(lambda part: lax.all_gather(part, axis), shard)  69.6 us
    psum x2, blocking collectives, frame_totals(): frame = lax.psum(terms, 'band')  46.4 us
  transfers between devices with their start and end apart: 6, of which 4 were waited for; matrix products, arithmetic and copies ran while one was open for 2% of the time, Pallas kernels for 0%

commit v1 on v0

--- a/solution.py
+++ b/solution.py
@@ -201,7 +201,7 @@
         jnp.bfloat16
     )[None]
     kernel_terms = jnp.stack(kernel_row_slice).reshape(3, 3, width)
-    kernel_total = lax.psum(kernel_terms, ("tm", "band"))
+    kernel_total = lax.psum(lax.psum(kernel_terms, "tm"), "band")
     total_tokens = lax.axis_size("tm") * lax.axis_size("band") * count
     kernel_grad = kernel_total / math.sqrt(total_tokens)
     return (mixed_out, query_grad, key_grad, value_grad, kernel_grad)

time: 877 us -> 1030 us (1.17)
  blocking collectives: 281 us -> 432 us
    psum x1, blocking collectives: 107 us -> 250 us  [shards(): kernel_total = lax.psum(lax.psum(kernel_terms, 'tm'), 'band')]
  transfers between devices with their start and end apart: 6 -> 6, of which waited for: 4 -> 3; matrix products, arithmetic and copies ran while one was open for 2% -> 2% of each run, Pallas kernels for 0% -> 0%
where the time goes in v1:
time: 1030 us; the launch traced here: 1020 us
  blocking collectives  432 us (42%)
  waiting for transfers between devices  219 us (21%)
  other arithmetic  181 us (18%)
  local copies, waits for them, and re-layouts  145 us (14%)
  matrix products  15 us (1%)
  between operations  14.3 us (1%)
    psum x1, blocking collectives, shards(): kernel_total = lax.psum(lax.psum(kernel_terms, 'tm'), 'band')  250 us
    select_n x256, other arithmetic, step(): return jax.tree.map(lambda a, b: jnp.where(reached, a, b), new, before)  163 us
    psum x2, waiting for transfers between devices, frame_totals(): frame = lax.psum(terms, 'band')  150 us
    all_gather x2, blocking collectives, entering(): everything = jax.tree.map(lambda part: lax.all_gather(part, axis), shard)  135 us
    dynamic_slice x256, local copies, waits for them, and re-layouts, step(): new = combine(before, jax.tree.map(lambda part: part[at], everything))  104 us
    all_gather x2, waiting for transfers between devices, entering(): everything = jax.tree.map(lambda part: lax.all_gather(part, axis), shard)  69.6 us
    psum x2, blocking collectives, frame_totals(): frame = lax.psum(terms, 'band')  46.4 us
  transfers between devices with their start and end apart: 6, of which 3 were waited for; matrix products, arithmetic and copies ran while one was open for 2% of the time, Pallas kernels for 0%

profile of v1, /device:TPU:1, one launch (start us, length us, event | category | flops | bytes accessed | tf_op | source)
XLA Modules:
  0.0 1016.0 jit_solution(2246477865476165636)
XLA Ops:
  7.2 1.5 reshape_reshape_squeeze.3
  10.0 2.6 reshape.180
  12.5 4.8 multiply_reduce_fusion.1
  17.4 79.9 %all-reduce.5.cloned.1.call-done = f32[35,32,32]{2,1,0:T(8,128)} async-done(((f32[35,32,32]{2,1,0:T(8,128)}), f32[35,32,32]{2,1,0:T(8,128)}) %all-reduce.5.cloned.1.call-update) | async-done | bytes 143376 | tf_op jit(solution)/shard_map/psum | solution.py:59
  98.4 22.5 %psum.43 = f32[35,32]{1,0:T(8,128)S(1)} all-reduce(f32[35,32]{1,0:T(8,128)S(1)} %reshape.182), channel_id=1, replica_groups=mesh['tm'=64,'band'=8] {'band'}, use_global_device_ids=true, to_apply=%region_3.4 | all-reduce | flops 1120 | bytes 8960 | tf_op jit(solution)/shard_map/psum | solution.py:59
  123.8 69.4 %all-gather.4 = f32[64,35,32]{1,2,0:T(8,128)} all-gather(f32[1,35,32]{1,2,0:T(8,128)S(1)} %copy.44), channel_id=3, replica_groups=mesh['tm'=64,'band'=8] {'tm'}, dimensions={0}, use_global_device_ids=true | all-gather | bytes 291200 | tf_op jit(solution)/shard_map/all_gather | solution.py:13
  193.2 69.6 %all-gather.9.cloned.1.call-done = f32[2240,32,32]{2,1,0:T(8,128)} async-done(((f32[35,32,32]{2,1,0:T(8,128)}), f32[2240,32,32]{2,1,0:T(8,128)}) %all-gather.9.cloned.1.call-update) | async-done | bytes 9175056 | tf_op jit(solution)/shard_map/all_gather | solution.py:13
  262.7 135.1 %while.34 = (s32[]{:T(128)}, f32[35,32,32]{2,1,0:T(8,128)S(1)}, f32[35,32]{1,0:T(8,128)S(1)}, s32[]{:T(128)}, f32[64,35,32,32]{3,2,1,0:T(8,128)}, /*index=5*/f32[64,35,32]{1,2,0:T(8,128)}, s32[]{:T(128)}, s32[]{:T(128)}) while((s32[]{:T(128)}, f32[35,32,32]{2,1,0:T(8,128)S(1)}, f32[35,32]{1,0:T(8,128)S(1)}, s32[]{:T(128)}, ...), condition=%wide.region_5.6_spmd.clone, body=%wide.region_4.5_spmd.clone.sunk | while | flops 110884 | bytes 461563 | solution.py:26
  397.9 2.4 mul.264
  400.3 3.6 mul.265
  405.8 2.4 reshape.183
  409.1 3.0 fusion.73
  412.2 1.5 reshape.185
  413.7 2.0 fusion.49
  415.7 3.9 reshape.187
  419.5 4.8 multiply_reduce_fusion
  424.4 70.0 %all-reduce.7.cloned.1.call-done = f32[35,32,32]{2,1,0:T(8,128)} async-done(((f32[35,32,32]{2,1,0:T(8,128)}), f32[35,32,32]{2,1,0:T(8,128)}) %all-reduce.7.cloned.1.call-update) | async-done | bytes 143376 | tf_op jit(solution)/shard_map/psum | solution.py:59
  496.7 4.2 collective-permute-start
  501.0 2.0 select_n.142
  503.1 1.5 fusion.10
  505.7 250.5 %psum.46 = f32[3,3,1120]{2,1,0:T(4,128)S(1)} all-reduce(f32[3,3,1120]{2,1,0:T(4,128)S(1)} %reshape.191), channel_id=1, replica_groups=mesh['tm'=64,'band'=8] {'tm'}, use_global_device_ids=true, to_apply=%region_21.22 | all-reduce | flops 10080 | bytes 80640 | tf_op jit(solution)/shard_map/psum | solution.py:204
  756.2 2.0 reshape.184
  758.2 2.8 convolution_bitcast_fusion.3
  762.3 2.5 reshape.186
  764.7 2.2 fusion.4
  768.6 23.9 %all-reduce.1 = (f32[35,32]{1,0:T(8,128)S(1)}, f32[3,3,1120]{2,1,0:T(4,128)S(1)}) all-reduce(f32[35,32]{1,0:T(8,128)S(1)} %reshape.189, f32[3,3,1120]{2,1,0:T(4,128)S(1)} %psum.46), channel_id=1, replica_groups=mesh['tm'=64,'band'=8] {'band'}, use_global_device_ids=true, to_apply=%region_9.10 | all-reduce | flops 11200 | bytes 89600 | tf_op jit(solution)/shard_map/psum | solution.py:59
  792.6 65.7 %all-gather.5 = f32[64,35,32]{1,2,0:T(8,128)} all-gather(f32[1,35,32]{1,2,0:T(8,128)S(1)} %copy.52), channel_id=5, replica_groups=mesh['tm'=64,'band'=8] {'tm'}, dimensions={0}, use_global_device_ids=true | all-gather | bytes 291200 | tf_op jit(solution)/shard_map/all_gather | solution.py:13
  860.3 135.5 %while.35 = (s32[]{:T(128)}, f32[35,32,32]{2,1,0:T(8,128)S(1)}, f32[35,32]{1,0:T(8,128)S(1)}, s32[]{:T(128)}, f32[64,35,32,32]{3,2,1,0:T(8,128)}, /*index=5*/f32...) while((s32[]{:T(128)}, f32[35,32,32]{2,1,0:T(8,128)S(1)}, ...), condition=%wide.region_11.12_spmd.clone, body=%wide.region_10.11_spmd.clone.sunk | while | flops 110888 | bytes 461625 | solution.py:26
  996.0 2.4 mul.306
  998.3 3.6 mul.307
  1003.0 1.5 convolution_bitcast_fusion
  1008.1 1.4 fusion.53
  (624 shorter events, 288.5 us)
Async XLA Ops:
  7.2 1.6 copy-start.18
  7.2 90.1 %all-reduce.5.cloned.1.call-start = ((), (), s32[]{:S(2)}) async-start(), calls=%async_computation | async-start | bytes 1146880 | tf_op jit(solution)/shard_map/psum | solution.py:59
  8.7 1.2 copy-start.5
  9.5 3.0 copy-start.7
  17.3 80.1 %copy-start.3 = (bf16[1,5,26,1120]{3,2,1,0:T(8,128)(2,1)S(1)}, bf16[1,5,26,1120]{3,2,1,0:T(8,128)(2,1)}, u32[]{:S(2)}) copy-start(bf16[1,5,26,1120]{3,2,1,0:T(8,128)(2,1)} %param.12) | copy-start | bytes 873604
  17.3 245.4 %all-gather.9.cloned.1.call-start = ((), (), s32[]{:S(2)}) async-start(), calls=%async_computation.2 | async-start | bytes 37273600 | tf_op jit(solution)/shard_map/all_gather | solution.py:13
  97.3 397.1 %all-reduce.7.cloned.1.call-start = ((), (), s32[]{:S(2)}) async-start(), calls=%async_computation.1 | async-start | bytes 1146880 | tf_op jit(solution)/shard_map/psum | solution.py:59
  98.3 23.0 %copy-start.20 = (bf16[1,5,26,1120]{3,2,1,0:T(8,128)(2,1)S(1)}, bf16[1,5,26,1120]{3,2,1,0:T(8,128)(2,1)}, u32[]{:S(2)}) copy-start(bf16[1,5,26,1120]{3,2,1,0:T(8,128)(2,1)} %param.9) | copy-start | bytes 873604
  123.7 284.6 %copy-start.1 = (f32[130,1120]{1,0:T(8,128)}, f32[130,1120]{1,0:T(8,128)S(1)}, u32[]{:S(2)}) copy-start(f32[130,1120]{1,0:T(8,128)S(1)} %reshape.192) | copy-start | bytes 1747204
  262.7 135.1 %copy-start.16 = (f32[35,32,32]{2,1,0:T(8,128)S(1)}, f32[35,32,32]{2,1,0:T(8,128)}, u32[]{:S(2)}) copy-start(f32[35,32,32]{2,1,0:T(8,128)} %all-reduce.5.cloned.1.call-done) | copy-start | bytes 430084
  400.3 3.6 copy-start.9
  412.2 1.5 copy-start.10
  413.7 5.8 copy-start
  424.3 70.1 %copy-start.17 = (bf16[1,5,26,1120]{3,2,1,0:T(8,128)(2,1)S(1)}, bf16[1,5,26,1120]{3,2,1,0:T(8,128)(2,1)}, u32[]{:S(2)}) copy-start(bf16[1,5,26,1120]{3,2,1,0:T(8,128)(2,1)} %param.11) | copy-start | bytes 873604
  424.4 435.9 %all-gather.11.cloned.1.call-start = ((), (), s32[]{:S(2)}) async-start(), calls=%async_computation.3 | async-start | bytes 37273600 | tf_op jit(solution)/shard_map/all_gather | solution.py:13
  494.5 0.9 copy-start.12
  495.4 7.6 copy-start.21
  495.4 7.7 collective-permute-start.1
  496.7 6.4 collective-permute-start
  762.3 4.6 copy-start.2
  764.7 2.2 copy-start.13
  764.7 2.2 copy-start.14
  767.7 91.2 %copy-start.4 = (f32[5,26,1120]{2,1,0:T(8,128)S(1)}, f32[5,26,1120]{2,1,0:T(8,128)}, u32[]{:S(2)}) copy-start(f32[5,26,1120]{2,1,0:T(8,128)} %reshape.184) | copy-start | bytes 1747204
  860.3 135.6 %copy-start.15 = (f32[35,32,32]{2,1,0:T(8,128)S(1)}, f32[35,32,32]{2,1,0:T(8,128)}, u32[]{:S(2)}) copy-start(f32[35,32,32]{2,1,0:T(8,128)} %all-reduce.7.cloned.1.call-done) | copy-start | bytes 430084
  998.3 3.6 copy-start.6
  1001.9 1.0 copy-start.8
  1004.8 1.1 copy-start.11
  1006.1 1.0 copy-start.19
Sparse Core Ops, SparseCore 0:
  17.5 79.7 all-reduce.4
  100.6 162.1 all-gather.8
  424.5 69.8 all-reduce.6
  497.5 161.5 all-gather.10
